TPU v7x, 32 devices: a whole 2x2x4 slice. The times are simulated.
32 devices in a mesh: row: 4 (over x, core), col: 8 (over z, y).
Axes of the slice: x: 2, y: 2, z: 4, core: 2. Of those that a mesh axis runs over, the one named last changes fastest.
Arguments:
- iterate: bfloat16 [4096, 8192], P('row', 'col'), may hold values from -0.5 to 0.5, as said below
Outputs:
- update: float32 [4096, 8192], P('row', 'col')
Inputs may be any that keep to these rules, and one draw needn't show every extreme that they name: One iterate of the orthogonalization.
All inputs are finite; a program needn't handle non-finite values.
Results may differ from a plain program's by a relative error of at most 0.0041.
Values may be sent and summed in bfloat16 or wider, within the bound.
A program may use at most 64 MiB of HBM per device.

v0:
```python
import math
import jax
import jax.numpy as jnp
from jax import lax
from jax.sharding import PartitionSpec as P

COLS = 8192
coef_a = 3.4445
coef_b = -4.775
coef_c = 2.0315


def per_device(iterate):
    cols_x = lax.all_gather(iterate, "row", axis=0, tiled=True)
    mirrored = lax.psum_scatter(
        lax.dot_general(
            cols_x, iterate, (((1,), (1,)), ((), ())), preferred_element_type=jnp.float32
        ),
        "col",
        scatter_dimension=0,
        tiled=True,
    )
    gram_block = mirrored.T.astype(jnp.bfloat16)
    gram_cols = lax.all_gather(gram_block, "row", axis=0, tiled=True)
    lower = gram_cols
    square = jnp.dot(
        lax.all_gather(gram_block, "col", axis=1, tiled=True),
        lower,
        preferred_element_type=jnp.float32,
    )
    poly = (coef_b * gram_block.astype(jnp.float32) + coef_c * square).astype(jnp.bfloat16)
    lower = cols_x
    mixed = jnp.dot(
        lax.all_gather(poly, "col", axis=1, tiled=True), lower, preferred_element_type=jnp.float32
    )
    return math.sqrt(COLS) * (coef_a * iterate.astype(jnp.float32) + mixed)


def solution(mesh):
    placed = (P("row", "col"),)
    return jax.shard_map(
        per_device, mesh=mesh, in_specs=placed, out_specs=P("row", "col"), check_vma=False
    )
```

profile of v0, /device:TPU:0, one launch (start us, length us, event | category | flops | bytes accessed | tf_op | source)
XLA Modules:
  0.0 684.1 jit_solution(4347285785540661950)
XLA Ops:
  6.5 0.0 all-gather.5.cloned.1.call-start
  6.5 0.7 all-gather.5.cloned.1.call-update
  7.3 0.0 reduce-scatter.2.cloned.1.call-start
  7.3 62.6 %all-gather.5.cloned.1.call-done = bf16[4096,1024]{1,0:T(8,128)(2,1)} async-done(((bf16[1024,1024]{1,0:T(8,128)(2,1)}), bf16[4096,1024]{1,0:T(8,128)(2,1)}) %all-gather.5.cloned.1.call-update) | async-done | bytes 8388624 | tf_op jit(solution)/shard_map/all_gather | solution.py:14
  69.9 16.1 %fusion = f32[4096,1024]{1,0:T(8,128)} fusion(bf16[4096,1024]{1,0:T(8,128)(2,1)} %all-gather.5.cloned.1.call-done, bf16[1024,1024]{1,0:T(8,128)(2,1)} %param.1), kind=kOutput, calls=%fused_computation.3 | convolution fusion | flops 8589934592 | bytes 27262976 | tf_op jit(solution)/shard_map/dot_general | solution.py:16
  86.1 0.0 reduce-scatter.2.cloned.1.call-update
  86.1 0.0 all-gather.9.cloned.1.call-start
  86.1 280.3 %reduce-scatter.2.cloned.1.call-done = f32[512,1024]{1,0:T(8,128)} async-done(((f32[4096,1024]{1,0:T(8,128)}), f32[512,1024]{1,0:T(8,128)}) %reduce-scatter.2.cloned.1.call-update) | async-done | bytes 2097168 | tf_op jit(solution)/shard_map/reduce_scatter | solution.py:15
  366.5 2.7 convert_bitcast_fusion
  369.2 0.0 all-gather.9.cloned.1.call-update
  369.2 0.0 all-gather.7.cloned.1.call-start
  369.2 0.5 all-gather.7.cloned.1.call-update
  369.8 0.0 copy-start
  369.8 0.0 all-gather.11.cloned.1.call-start
  369.8 33.1 %all-gather.9.cloned.1.call-done = bf16[4096,512]{0,1:T(8,128)(2,1)} async-done(((bf16[1024,512]{0,1:T(8,128)(2,1)}), bf16[4096,512]{0,1:T(8,128)(2,1)}) %all-gather.9.cloned.1.call-update) | async-done | bytes 4194320 | tf_op jit(solution)/shard_map/all_gather | solution.py:24
  402.9 126.5 %all-gather.7.cloned.1.call-done = bf16[1024,4096]{0,1:T(8,128)(2,1)} async-done(((bf16[1024,512]{0,1:T(8,128)(2,1)}), bf16[1024,4096]{0,1:T(8,128)(2,1)}) %all-gather.7.cloned.1.call-update) | async-done | bytes 8388624 | tf_op jit(solution)/shard_map/all_gather | solution.py:27
  529.4 10.3 %add_convert_fusion = bf16[1024,512]{0,1:T(8,128)(2,1)} fusion(bf16[1024,512]{0,1:T(8,128)(2,1)} %convert_bitcast_fusion, bf16[4096,512]{0,1:T(8,128)(2,1)} %all-gather.9.cloned.1.call-done, bf16[1024,4096]{0,1:T(8,128)(2,1)} %all-gather.7.cloned.1.call-done), kind=kOutput, calls=%fused_computation.1 | convolution fusion | flops 4297588736 | bytes 14680064 | tf_op jit(solution)/shard_map/dot_general | solution.py:26
  539.7 0.0 all-gather.11.cloned.1.call-update
  539.7 122.8 %all-gather.11.cloned.1.call-done = bf16[1024,4096]{0,1:T(8,128)(2,1)} async-done(((bf16[1024,512]{0,1:T(8,128)(2,1)}), bf16[1024,4096]{0,1:T(8,128)(2,1)}) %all-gather.11.cloned.1.call-update) | async-done | bytes 8388624 | tf_op jit(solution)/shard_map/all_gather | solution.py:34
  662.5 0.0 copy-done
  662.5 15.1 %add_multiply_fusion = f32[1024,1024]{1,0:T(8,128)} fusion(bf16[1024,1024]{1,0:T(8,128)(2,1)S(1)} %copy-done, bf16[1024,4096]{0,1:T(8,128)(2,1)} %all-gather.11.cloned.1.call-done, bf16[4096,1024]{1,0:T(8,128)(2,1)} %all-gather.5.cloned.1.call-done), kind=kOutput, calls=%fused_computation | convolution fusion | flops 8594128896 | bytes 23068672 | tf_op jit(solution)/shard_map/dot_general | solution.py:33
Async XLA Ops:
  6.5 63.4 %all-gather.5.cloned.1.call-start = ((), (), s32[]{:S(2)}) async-start(), calls=%async_computation.1 | async-start | bytes 10485760 | tf_op jit(solution)/shard_map/all_gather | solution.py:14
  7.3 359.2 %reduce-scatter.2.cloned.1.call-start = ((), (), s32[]{:S(2)}) async-start(), calls=%async_computation.2 | async-start | bytes 18874368 | tf_op jit(solution)/shard_map/reduce_scatter | solution.py:15
  86.1 316.8 %all-gather.9.cloned.1.call-start = ((), (), s32[]{:S(2)}) async-start(), calls=%async_computation.4 | async-start | bytes 5242880 | tf_op jit(solution)/shard_map/all_gather | solution.py:24
  369.2 160.2 %all-gather.7.cloned.1.call-start = ((), (), s32[]{:S(2)}) async-start(), calls=%async_computation.3 | async-start | bytes 9437184 | tf_op jit(solution)/shard_map/all_gather | solution.py:27
  369.8 292.8 %copy-start = (bf16[1024,1024]{1,0:T(8,128)(2,1)S(1)}, bf16[1024,1024]{1,0:T(8,128)(2,1)}, u32[]{:S(2)}) copy-start(bf16[1024,1024]{1,0:T(8,128)(2,1)} %param.1) | copy-start | bytes 6291460
  369.8 292.7 %all-gather.11.cloned.1.call-start = ((), (), s32[]{:S(2)}) async-start(), calls=%async_computation.5 | async-start | bytes 9437184 | tf_op jit(solution)/shard_map/all_gather | solution.py:34
Sparse Core Ops, SparseCore 0:
  8.9 60.9 all-gather.4
  86.2 280.2 reduce-scatter.1
  369.3 33.5 all-gather.8
  404.9 124.4 all-gather.6
  539.8 122.6 all-gather.10
where the time goes:
time: 684 us
  waiting for transfers between devices  627 us (92%)
  matrix products  41.5 us (6%)
  between operations  13.1 us (2%)
    reduce_scatter x1, waiting for transfers between devices, per_device(): lax.psum_scatter(lax.dot_general(cols_x, iterate, (((1,), (1,)), ((), ())...  280 us
    all_gather x1, waiting for transfers between devices, per_device(): lax.all_gather(gram_block, 'col', axis=1, tiled=True)  126 us
    all_gather x1, waiting for transfers between devices, per_device(): lax.all_gather(poly, 'col', axis=1, tiled=True)  123 us
    all_gather x1, waiting for transfers between devices, per_device(): cols_x = lax.all_gather(iterate, 'row', axis=0, tiled=True)  62.6 us
    all_gather x1, waiting for transfers between devices, per_device(): gram_cols = lax.all_gather(gram_block, 'row', axis=0, tiled=True)  33.1 us
    dot_general x1, matrix products, per_device(): lax.dot_general(cols_x, iterate, (((1,), (1,)), ((), ())), preferred_elem...  16.1 us
    dot_general x1, matrix products, per_device(): jnp.dot(lax.all_gather(poly, 'col', axis=1, tiled=True), lower, preferred...  15.1 us
  transfers between devices with their start and end apart: 5, of which 5 were waited for; matrix products, arithmetic and copies ran while one was open for 0% of the time, Pallas kernels for 0%

commit v1 on v0

--- a/solution.py
+++ b/solution.py
@@ -11,7 +11,12 @@
 
 
 def per_device(iterate):
-    cols_x = lax.all_gather(iterate, "row", axis=0, tiled=True)
+    ring = [iterate]
+    for hop in range(3):
+        ring.append(lax.ppermute(ring[-1], "row", [(dev, (dev + 1) % 4) for dev in range(4)]))
+    cols_x = jnp.roll(
+        jnp.concatenate(ring[::-1], axis=0), (lax.axis_index("row") + 1) * ring[0].shape[0], axis=0
+    )
     mirrored = lax.psum_scatter(
         lax.dot_general(
             cols_x, iterate, (((1,), (1,)), ((), ())), preferred_element_type=jnp.float32

time: 684 us -> 711 us (1.039)
  waiting for transfers between devices: 627 us -> 643 us
  local copies, waits for them, and re-layouts: 0.01 us -> 14.8 us
    ppermute x0 -> x3, waiting for transfers between devices: none -> 77.2 us  [per_device(): lax.ppermute(ring[-1], 'row', [(dev, (dev + 1) % 4) for dev in range(4)])]
    all_gather x1 -> x0, waiting for transfers between devices: 62.6 us -> none  [per_device(): cols_x = lax.all_gather(iterate, 'row', axis=0, tiled=True)]
    unnamed x2 -> x15, local copies, waits for them, and re-layouts: 0.01 us -> 14.6 us
  transfers between devices with their start and end apart: 5 -> 7, of which waited for: 5 -> 7; matrix products, arithmetic and copies ran while one was open for 0% -> 0% of each run, Pallas kernels for 0% -> 0%
where the time goes in v1:
time: 711 us
  waiting for transfers between devices  643 us (90%)
  matrix products  37.2 us (5%)
  local copies, waits for them, and re-layouts  14.8 us (2%)
  between operations  13.2 us (2%)
    reduce_scatter x1, waiting for transfers between devices, per_device(): lax.psum_scatter(lax.dot_general(cols_x, iterate, (((1,), (1,)), ((), ())...  282 us
    all_gather x1, waiting for transfers between devices, per_device(): lax.all_gather(gram_block, 'col', axis=1, tiled=True)  127 us
    all_gather x1, waiting for transfers between devices, per_device(): lax.all_gather(poly, 'col', axis=1, tiled=True)  123 us
    ppermute x3, waiting for transfers between devices, per_device(): lax.ppermute(ring[-1], 'row', [(dev, (dev + 1) % 4) for dev in range(4)])  77.2 us
    all_gather x1, waiting for transfers between devices, per_device(): gram_cols = lax.all_gather(gram_block, 'row', axis=0, tiled=True)  32.9 us
    dot_general x1, matrix products, per_device(): jnp.dot(lax.all_gather(poly, 'col', axis=1, tiled=True), lower, preferred...  15.1 us
    unnamed x15, local copies, waits for them, and re-layouts  14.6 us
  transfers between devices with their start and end apart: 7, of which 7 were waited for; matrix products, arithmetic and copies ran while one was open for 0% of the time, Pallas kernels for 0%

profile of v1, /device:TPU:0, one launch (start us, length us, event | category | flops | bytes accessed | tf_op | source)
XLA Modules:
  0.0 711.2 jit_solution(11976273718335008930)
XLA Ops:
  6.5 0.0 reduce-scatter.2.cloned.1.call-start
  6.5 0.5 collective-permute-start
  7.0 25.9 %collective-permute-done = bf16[1024,1024]{1,0:T(8,128)(2,1)S(1)} collective-permute-done((bf16[1024,1024]{1,0:T(8,128)(2,1)}, bf16[1024,1024]{1,0:T(8,128)(2,1)S(1)}, u32[]{:S(2)}, u32[]{:S(2)}) %collective-permute-start) | collective-permute-done | bytes 2097184 | tf_op jit(solution)/shard_map/ppermute | solution.py:16
  32.9 1.3 copy-done.1
  34.3 0.0 collective-permute-start.1
  34.3 25.6 %collective-permute-done.1 = bf16[1024,1024]{1,0:T(8,128)(2,1)} collective-permute-done((bf16[1024,1024]{1,0:T(8,128)(2,1)S(1)}, bf16[1024,1024]{1,0:T(8,128)(2,1)}, u32[]{:S(2)}, u32[]{:S(2)}) %collective-permute-start.1) | collective-permute-done | bytes 2097184 | tf_op jit(solution)/shard_map/ppermute | solution.py:16
  59.8 0.0 collective-permute-start.2
  59.8 25.8 %collective-permute-done.2 = bf16[1024,1024]{1,0:T(8,128)(2,1)} collective-permute-done((bf16[1024,1024]{1,0:T(8,128)(2,1)}, bf16[1024,1024]{1,0:T(8,128)(2,1)}, u32[]{:S(2)}, u32[]{:S(2)}) %collective-permute-start.2) | collective-permute-done | bytes 2097184 | tf_op jit(solution)/shard_map/ppermute | solution.py:16
  85.6 1.8 constant_dynamic-update-slice_fusion.7
  87.4 1.8 constant_dynamic-update-slice_fusion.6
  89.1 0.2 constant_dynamic-update-slice_fusion.5
  89.3 0.2 constant_dynamic-update-slice_fusion.4
  89.5 1.8 constant_dynamic-update-slice_fusion.3
  91.3 1.8 constant_dynamic-update-slice_fusion.2
  93.0 0.2 constant_dynamic-update-slice_fusion.1
  93.2 0.2 constant_dynamic-update-slice_fusion
  93.4 5.7 copy-done.3
  99.2 11.8 %fusion.2 = f32[4096,1024]{1,0:T(8,128)} fusion(bf16[1024,1024]{1,0:T(8,128)(2,1)S(1)} %copy-done, bf16[8192,1024]{1,0:T(8,128)(2,1)S(1)} %constant_dynamic-update-slice_fusion, s32[]{:T(128)S(6)} %select_n.14), kind=kOutput, calls=%fused_computation.2 | convolution fusion | flops 8589934592 | bytes 27262980 | tf_op jit(solution)/shard_map/dot_general | solution.py:21
  111.0 0.0 reduce-scatter.2.cloned.1.call-update
  111.0 0.0 all-gather.6.cloned.1.call-start
  111.0 282.3 %reduce-scatter.2.cloned.1.call-done = f32[512,1024]{1,0:T(8,128)} async-done(((f32[4096,1024]{1,0:T(8,128)}), f32[512,1024]{1,0:T(8,128)}) %reduce-scatter.2.cloned.1.call-update) | async-done | bytes 2097168 | tf_op jit(solution)/shard_map/reduce_scatter | solution.py:20
  393.3 2.7 convert_bitcast_fusion
  396.0 0.0 all-gather.6.cloned.1.call-update
  396.1 0.0 all-gather.4.cloned.1.call-start
  396.1 0.7 all-gather.4.cloned.1.call-update
  396.8 0.0 all-gather.8.cloned.1.call-start
  396.9 32.9 %all-gather.6.cloned.1.call-done = bf16[4096,512]{0,1:T(8,128)(2,1)} async-done(((bf16[1024,512]{0,1:T(8,128)(2,1)}), bf16[4096,512]{0,1:T(8,128)(2,1)}) %all-gather.6.cloned.1.call-update) | async-done | bytes 4194320 | tf_op jit(solution)/shard_map/all_gather | solution.py:29
  429.8 126.6 %all-gather.4.cloned.1.call-done = bf16[1024,4096]{0,1:T(8,128)(2,1)} async-done(((bf16[1024,512]{0,1:T(8,128)(2,1)}), bf16[1024,4096]{0,1:T(8,128)(2,1)}) %all-gather.4.cloned.1.call-update) | async-done | bytes 8388624 | tf_op jit(solution)/shard_map/all_gather | solution.py:32
  556.4 10.3 %add_convert_fusion = bf16[1024,512]{0,1:T(8,128)(2,1)} fusion(bf16[1024,512]{0,1:T(8,128)(2,1)} %convert_bitcast_fusion, bf16[4096,512]{0,1:T(8,128)(2,1)} %all-gather.6.cloned.1.call-done, bf16[1024,4096]{0,1:T(8,128)(2,1)} %all-gather.4.cloned.1.call-done), kind=kOutput, calls=%fused_computation.5 | convolution fusion | flops 4297588736 | bytes 14680064 | tf_op jit(solution)/shard_map/dot_general | solution.py:31
  566.7 0.0 all-gather.8.cloned.1.call-update
  566.7 122.8 %all-gather.8.cloned.1.call-done = bf16[1024,4096]{0,1:T(8,128)(2,1)} async-done(((bf16[1024,512]{0,1:T(8,128)(2,1)}), bf16[1024,4096]{0,1:T(8,128)(2,1)}) %all-gather.8.cloned.1.call-update) | async-done | bytes 8388624 | tf_op jit(solution)/shard_map/all_gather | solution.py:39
  689.5 15.1 %add_multiply_fusion = f32[1024,1024]{1,0:T(8,128)} fusion(bf16[1024,1024]{1,0:T(8,128)(2,1)S(1)} %copy-done, bf16[1024,4096]{0,1:T(8,128)(2,1)} %all-gather.8.cloned.1.call-done, bf16[8192,1024]{1,0:T(8,128)(2,1)} %copy-done.3, s32[]{:T(128)S(6)} %select_n.14), kind=kOutput, calls=%fused_computation.4 | convolution fusion | flops 8594128896 | bytes 23068676 | tf_op jit(solution)/shard_map/dot_general | solution.py:38
  (6 shorter events, 0.0 us)
Async XLA Ops:
  6.5 82.8 %copy-start = (bf16[1024,1024]{1,0:T(8,128)(2,1)S(1)}, bf16[1024,1024]{1,0:T(8,128)(2,1)}, u32[]{:S(2)}) copy-start(bf16[1024,1024]{1,0:T(8,128)(2,1)} %param.1) | copy-start | bytes 6291460
  6.5 386.8 %reduce-scatter.2.cloned.1.call-start = ((), (), s32[]{:S(2)}) async-start(), calls=%async_computation.1 | async-start | bytes 18874368 | tf_op jit(solution)/shard_map/reduce_scatter | solution.py:20
  6.5 26.4 %collective-permute-start = (bf16[1024,1024]{1,0:T(8,128)(2,1)}, bf16[1024,1024]{1,0:T(8,128)(2,1)S(1)}, u32[]{:S(2)}, u32[]{:S(2)}) collective-permute-start(bf16[1024,1024]{1,0:T(8,128)(2,1)} %param.1), channel_id=1, source_target_pairs={{0,8},{8,16},{16,24},{24,0},{1,9},{9,17},{17,25},{25,1},{2,10},{10... | collective-permute-start | bytes 6291464 | tf_op jit(solution)/shard_map/ppermute | solution.py:16
  32.9 1.3 copy-start.1
  34.3 25.6 %collective-permute-start.1 = (bf16[1024,1024]{1,0:T(8,128)(2,1)S(1)}, bf16[1024,1024]{1,0:T(8,128)(2,1)}, u32[]{:S(2)}, u32[]{:S(2)}) collective-permute-start(bf16[1024,1024]{1,0:T(8,128)(2,1)S(1)} %collective-permute-done), channel_id=1, source_target_pairs={{0,8},{8,16},{16,24},{24,0},{1,9},{9,17},{17,25},{25,1},{2,10},{10... | collective-permute-start | bytes 6291464 | tf_op jit(solution)/shard_map/ppermute | solution.py:16
  59.8 25.8 %collective-permute-start.2 = (bf16[1024,1024]{1,0:T(8,128)(2,1)}, bf16[1024,1024]{1,0:T(8,128)(2,1)}, u32[]{:S(2)}, u32[]{:S(2)}) collective-permute-start(bf16[1024,1024]{1,0:T(8,128)(2,1)} %collective-permute-done.1), channel_id=1, source_target_pairs={{0,8},{8,16},{16,24},{24,0},{1,9},{9,17},{17,25},{25,1},{2,10},{10... | collective-permute-start | bytes 6291464 | tf_op jit(solution)/shard_map/ppermute | solution.py:16
  59.8 29.3 %copy-start.2 = (bf16[1024,1024]{1,0:T(8,128)(2,1)S(1)}, bf16[1024,1024]{1,0:T(8,128)(2,1)}, u32[]{:S(2)}) copy-start(bf16[1024,1024]{1,0:T(8,128)(2,1)} %copy-done.1) | copy-start | bytes 6291460
  93.4 5.7 copy-start.3
  111.0 318.8 %all-gather.6.cloned.1.call-start = ((), (), s32[]{:S(2)}) async-start(), calls=%async_computation.3 | async-start | bytes 5242880 | tf_op jit(solution)/shard_map/all_gather | solution.py:29
  396.1 160.3 %all-gather.4.cloned.1.call-start = ((), (), s32[]{:S(2)}) async-start(), calls=%async_computation.2 | async-start | bytes 9437184 | tf_op jit(solution)/shard_map/all_gather | solution.py:32
  396.8 292.7 %all-gather.8.cloned.1.call-start = ((), (), s32[]{:S(2)}) async-start(), calls=%async_computation.4 | async-start | bytes 9437184 | tf_op jit(solution)/shard_map/all_gather | solution.py:39
Sparse Core Ops, SparseCore 0:
  111.1 282.1 reduce-scatter.1
  396.2 33.5 all-gather.5
  431.9 124.4 all-gather.3
  566.9 122.6 all-gather.7
